TPU v7x, 32 devices: a whole 2x2x4 slice. The times are simulated.
32 devices in a mesh: det: 4 (over y, x), obs: 8 (over z, core).
Axes of the slice: x: 2, y: 2, z: 4, core: 2. Of those that a mesh axis runs over, the one named last changes fastest.
Arguments:
- tod: float32 [4, 8, 8192], P('det', 'obs'), may hold values from -200 to 200
- angle: float32 [4, 8, 8192], P('det', 'obs'), may hold values from -3.140625 to 3.140625
- pix_in: int32 [4, 8, 8192], P('det', 'obs'), may hold values from 0 to 63
- tile_block: int32 [4, 8, 32], P('det', 'obs'), may hold values from 0 to 511
- base_len: int32 [4, 8, 40], P('det', 'obs'), may hold values from 1 to 384, 8192 in all within a row
- touched: int32 [8, 16], P('obs'), may hold values from 0 to 511, as said below
Outputs:
- baselines: float32 [4, 8, 40], P('det', 'obs')
- residual_rate: float32 [4, 8, 40], P('det', 'obs')
Inputs may be any that keep to these rules, and one draw needn't show every extreme that they name: `touched`: each row lists 16 distinct patches; patch p is held by owner p // 64; at most 4 patches of one row share an owner, and one owner holds exactly 4 patches of every row.
All inputs are finite; a program needn't handle non-finite values.
Results may differ from a plain program's by a relative error of at most 0.0003.
Values sent between devices are 32-bit elements; how exact they have to be, the bound alone decides.
A program may use at most 128 MiB of HBM per device.

v0:
```python
import math

import jax
import jax.numpy as jnp
from jax import lax
from jax.sharding import PartitionSpec as P

TILE = 256
BLK = 64
PATCH_PIX = 2048
PT = 16
PATCH_OWN = 64
ITERS = 2


UPPER_LIMIT = lax.Precision.HIGHEST


def pixel_inverse(hits):
    a11 = hits[:, 0] + 1.0
    a12 = hits[:, 1]
    a13 = hits[:, 2]
    a22 = hits[:, 3] + 1.0
    a23 = hits[:, 4]
    a33 = hits[:, 5] + 1.0
    c11 = a22 * a33 - a23 * a23
    c12 = a13 * a23 - a12 * a33
    c13 = a12 * a23 - a13 * a22
    c22 = a11 * a33 - a13 * a13
    c23 = a12 * a13 - a11 * a23
    c33 = a11 * a22 - a12 * a12
    determinant = a11 * c11 + a12 * c12 + a13 * c13
    return jnp.stack([c11, c12, c13, c22, c23, c33], axis=1) / determinant[:, None]


def apply_inverse(inverse, pixel_binned_map):
    first = (
        inverse[:, 0] * pixel_binned_map[:, 0]
        + inverse[:, 1] * pixel_binned_map[:, 1]
        + inverse[:, 2] * pixel_binned_map[:, 2]
    )
    second = (
        inverse[:, 1] * pixel_binned_map[:, 0]
        + inverse[:, 3] * pixel_binned_map[:, 1]
        + inverse[:, 4] * pixel_binned_map[:, 2]
    )
    third = (
        inverse[:, 2] * pixel_binned_map[:, 0]
        + inverse[:, 4] * pixel_binned_map[:, 1]
        + inverse[:, 5] * pixel_binned_map[:, 2]
    )
    return jnp.stack([first, second, third], axis=1)


def combine_det(partial_value):
    total = lax.psum(partial_value, "det")
    return total


def squares(residual_vector):
    return lax.psum(jnp.sum(residual_vector * residual_vector), ("det", "obs"))


def body(tod, angle, pix_in, tile_block, base_len, touched):
    signal = tod[0, 0]
    inner = pix_in[0, 0]
    tile_rows = tile_block[0, 0]
    lengths = base_len[0, 0]
    patch_list = touched[0]
    samples = signal.shape[0]
    nbase = lengths.shape[0]
    ntile = samples // TILE
    group = math.gcd(ntile, 64)
    groups = ntile // group
    blocks = PATCH_PIX // BLK
    local_blocks = PT * blocks
    obs_count = lax.axis_size("obs")
    cap = max(2, 2 * PT // obs_count)
    slots = obs_count * cap
    cos_w = jnp.cos(2.0 * angle[0, 0])
    sin_w = jnp.sin(2.0 * angle[0, 0])
    ends = jnp.cumsum(lengths)
    base_index = jnp.searchsorted(ends, jnp.arange(samples, dtype=jnp.int32), side="right")
    inner_groups = inner.reshape(groups, group, TILE)
    cos_groups = cos_w.reshape(groups, group, TILE)
    sin_groups = sin_w.reshape(groups, group, TILE)
    pixel_iota = jnp.arange(BLK, dtype=jnp.int32)
    tile_select = (tile_rows[None, :] == jnp.arange(local_blocks, dtype=jnp.int32)[:, None]).astype(
        jnp.float32
    )

    def tile_indicator_matrix(index):
        return (index[:, None, :] == pixel_iota[None, :, None]).astype(jnp.float32)

    def bin_local(value_entries):
        comps = value_entries.shape[0]
        grouped = value_entries.reshape(comps, groups, group, TILE).transpose(1, 2, 0, 3)

        def bin_one_group(index_couple):
            return jnp.einsum(
                "awv,agv->awg",
                index_couple[0],
                tile_indicator_matrix(index_couple[1]),
                precision=UPPER_LIMIT,
            )

        per_tile = lax.map(bin_one_group, (grouped, inner_groups)).reshape(ntile, comps * BLK)
        summed = jnp.dot(tile_select, per_tile, precision=UPPER_LIMIT)
        return (
            summed.reshape(PT, blocks, comps, BLK)
            .transpose(0, 2, 1, 3)
            .reshape(PT, comps, PATCH_PIX)
        )

    def unbin_local(local_map):
        rows = (
            local_map.reshape(PT, 3, blocks, BLK)
            .transpose(0, 2, 1, 3)
            .reshape(local_blocks, 3 * BLK)
        )
        picked = jnp.take(rows, tile_rows, axis=0).reshape(groups, group, 3, BLK)

        def unbin_one_group(partition_pieces):
            value_entries = jnp.einsum(
                "jwx,jxd->jwd",
                partition_pieces[0],
                tile_indicator_matrix(partition_pieces[1]),
                precision=UPPER_LIMIT,
            )
            return (
                value_entries[:, 0]
                + partition_pieces[2] * value_entries[:, 1]
                + partition_pieces[3] * value_entries[:, 2]
            )

        return lax.map(unbin_one_group, (picked, inner_groups, cos_groups, sin_groups)).reshape(
            samples
        )

    owner_of = patch_list // PATCH_OWN
    slot_of = patch_list % PATCH_OWN
    positions = jnp.arange(PT, dtype=jnp.int32)
    before = (owner_of[None, :] == owner_of[:, None]) & (positions[None, :] < positions[:, None])
    rank = jnp.sum(before.astype(jnp.int32), axis=1)
    target = owner_of * cap + rank
    placed = target[None, :] == jnp.arange(slots, dtype=jnp.int32)[:, None]
    packing = placed.astype(jnp.float32)
    send_ids = (jnp.sum(jnp.where(placed, slot_of[None, :] + 1, 0), axis=1) - 1).reshape(
        obs_count, cap
    )

    def pack_map(total):
        comps, width = (total.shape[1], total.shape[2])
        return jnp.dot(packing, total.reshape(PT, comps * width), precision=UPPER_LIMIT).reshape(
            obs_count, cap, comps, width
        )

    def unpack_map(returned):
        width = returned.shape[3]
        return jnp.dot(
            packing.T, returned.reshape(slots, 3 * width), precision=UPPER_LIMIT
        ).reshape(PT, 3, width)

    ones = jnp.ones_like(signal)
    first_values = jnp.stack(
        [
            signal,
            signal * cos_w,
            signal * sin_w,
            ones,
            cos_w,
            sin_w,
            cos_w * cos_w,
            cos_w * sin_w,
            sin_w * sin_w,
        ]
    )
    first_total = combine_det(bin_local(first_values))
    received, source_ids = (
        lax.all_to_all(pack_map(first_total), "obs", split_axis=0, concat_axis=0, tiled=True),
        lax.all_to_all(send_ids, "obs", split_axis=0, concat_axis=0, tiled=True),
    )
    owner_pick = (
        source_ids.reshape(slots)[None, :] == jnp.arange(PATCH_OWN, dtype=jnp.int32)[:, None]
    ).astype(jnp.float32)

    def gather_owner(arrived):
        comps, width = (arrived.shape[2], arrived.shape[3])
        return jnp.dot(
            owner_pick, arrived.reshape(slots, comps * width), precision=UPPER_LIMIT
        ).reshape(PATCH_OWN, comps, width)

    def return_map(owned):
        width = owned.shape[2]
        outgoing = jnp.dot(
            owner_pick.T, owned.reshape(PATCH_OWN, 3 * width), precision=UPPER_LIMIT
        ).reshape(obs_count, cap, 3, width)
        return lax.all_to_all(outgoing, "obs", split_axis=0, concat_axis=0, tiled=True)

    accumulated = gather_owner(received)
    inverse = pixel_inverse(accumulated[:, 3:])
    start_map = apply_inverse(inverse, accumulated[:, :3])
    start_local = unpack_map(return_map(start_map))
    cleaned = signal - unbin_local(start_local)
    right_side = jax.ops.segment_sum(
        cleaned, base_index, num_segments=nbase, indices_are_sorted=True
    )
    solution = jnp.zeros_like(right_side)
    residual_vector = right_side
    direction = right_side
    norm_now = squares(residual_vector)
    for step in range(ITERS):
        expanded = jnp.take(direction, base_index)
        apply_value_entries = jnp.stack([expanded, expanded * cos_w, expanded * sin_w])
        apply_total = combine_det(bin_local(apply_value_entries))
        apply_arrived = lax.all_to_all(
            pack_map(apply_total), "obs", split_axis=0, concat_axis=0, tiled=True
        )
        solved = apply_inverse(inverse, gather_owner(apply_arrived))
        apply_local_map = unpack_map(return_map(solved))
        image = jax.ops.segment_sum(
            expanded - unbin_local(apply_local_map),
            base_index,
            num_segments=nbase,
            indices_are_sorted=True,
        )
        alpha = norm_now / lax.psum(jnp.sum(direction * image), ("det", "obs"))
        solution = solution + alpha * direction
        residual_vector = residual_vector - alpha * image
        if step + 1 < ITERS:
            norm_next = squares(residual_vector)
            direction = residual_vector + norm_next / norm_now * direction
            norm_now = norm_next
    rate = residual_vector / lengths.astype(jnp.float32)
    return (solution[None, None], rate[None, None])


def solution(mesh):
    placed = (
        P("det", "obs", None),
        P("det", "obs", None),
        P("det", "obs", None),
        P("det", "obs", None),
        P("det", "obs", None),
        P("obs", None),
    )
    return jax.shard_map(
        body,
        mesh=mesh,
        in_specs=placed,
        out_specs=(P("det", "obs", None), P("det", "obs", None)),
        check_vma=False,
    )
```

profile of v0, /device:TPU:0, one launch (start us, length us, event | category | flops | bytes accessed | tf_op | source)
XLA Modules:
  0.0 1070.0 jit_solution(13468639081524979222)
XLA Ops:
  18.3 6.4 all-to-all-start
  24.7 49.8 %all-reduce.5.cloned.1.call-done = f32[9,2048,16]{1,2,0:T(8,128)} async-done(((f32[9,2048,16]{1,2,0:T(8,128)}), f32[9,2048,16]{1,2,0:T(8,128)}) %all-reduce.5.cloned.1.call-update) | async-done | bytes 1179664 | tf_op jit(solution)/shard_map/psum | solution.py:56
  74.5 4.4 fusion.34
  79.0 5.0 all-to-all-start.1
  85.2 53.4 %all-to-all-done.1 = f32[8,4,9,2048]{3,1,2,0:T(4,128)S(1)} async-done(((f32[8,4,9,2048]{3,1,2,0:T(4,128)}), f32[8,4,9,2048]{3,1,2,0:T(4,128)S(1)}, u32[]{:S(2)}, u32[]{:S(2)}) %all-to-all-start.1) | async-done | bytes 2359328 | tf_op jit(solution)/shard_map/all_to_all | solution.py:180
  151.7 312.5 %while.24 = (s32[]{:T(128)}, u32[8192]{0:T(1024)S(1)}, u32[8192]{0:T(1024)S(1)}, s32[40]{0:T(128)S(1)}, s32[]{:T(128)}, /*index=5*/s32[]{:T(128)}) while((s32[]{:T(128)}, u32[8192]{0:T(1024)S(1)}, u32[8192]{0:T(1024)S(1)}, s32[40]{0:T(128)S(1)}, s32[]{:T(128)}, /*index=5*/s32[]{:T(128)}) %tuple.233), condition=%wide.region_2.3_spmd.clone, body=%wide.region_1.2_spmd.clone.sunk | while | flops 1392643 | bytes 262864 | solution.py:83
  153.9 25.0 %fusion.141 = u32[8192]{0:T(1024)S(1)} fusion(u32[8192]{0:T(1024)S(1)} %get-tuple-element.525, u32[8192]{0:T(1024)S(1)} %get-tuple-element.524, s32[]{:T(128)} %bitcast.438, s32[]{:T(128)} %bitcast.439, s32[]{:T(128)} %bitcast.440, s32[]{:T(128)} %bitcast.441, s32[]{:T(128)} %bitcast.442, s32[]{:T(128)} %bitcast.443, s32[]{:T(128)} %bitcast.444, ...), kind=kLoop, calls=%fused_computation.8.clone.1 | loop fusion | flops 696320 | bytes 98465 | tf_op jit(solution)/shard_map/jit(searchsorted)/jit(_searchsorted_scan_impl)/vmap(jit(_searchsorted_scan_impl))/while/body/eval_jaxpr/select_n | solution.py:83
  178.8 25.0 %fusion.140 = u32[8192]{0:T(1024)S(1)} fusion(u32[8192]{0:T(1024)S(1)} %get-tuple-element.525, u32[8192]{0:T(1024)S(1)} %get-tuple-element.524, s32[]{:T(128)} %bitcast.438, s32[]{:T(128)} %bitcast.439, s32[]{:T(128)} %bitcast.440, s32[]{:T(128)} %bitcast.441, s32[]{:T(128)} %bitcast.442, s32[]{:T(128)} %bitcast.443, s32[]{:T(128)} %bitcast.444, ...), kind=kLoop, calls=%fused_computation.9.clone.1 | loop fusion | flops 696320 | bytes 98465 | tf_op jit(solution)/shard_map/jit(searchsorted)/jit(_searchsorted_scan_impl)/vmap(jit(_searchsorted_scan_impl))/while/body/eval_jaxpr/select_n | solution.py:83
  205.9 25.0 %fusion.141 = u32[8192]{0:T(1024)S(1)} fusion(u32[8192]{0:T(1024)S(1)} %get-tuple-element.525, u32[8192]{0:T(1024)S(1)} %get-tuple-element.524, s32[]{:T(128)} %bitcast.438, s32[]{:T(128)} %bitcast.439, s32[]{:T(128)} %bitcast.440, s32[]{:T(128)} %bitcast.441, s32[]{:T(128)} %bitcast.442, s32[]{:T(128)} %bitcast.443, s32[]{:T(128)} %bitcast.444, ...), kind=kLoop, calls=%fused_computation.8.clone.1 | loop fusion | flops 696320 | bytes 98465 | tf_op jit(solution)/shard_map/jit(searchsorted)/jit(_searchsorted_scan_impl)/vmap(jit(_searchsorted_scan_impl))/while/body/eval_jaxpr/select_n | solution.py:83
  230.9 25.0 %fusion.140 = u32[8192]{0:T(1024)S(1)} fusion(u32[8192]{0:T(1024)S(1)} %get-tuple-element.525, u32[8192]{0:T(1024)S(1)} %get-tuple-element.524, s32[]{:T(128)} %bitcast.438, s32[]{:T(128)} %bitcast.439, s32[]{:T(128)} %bitcast.440, s32[]{:T(128)} %bitcast.441, s32[]{:T(128)} %bitcast.442, s32[]{:T(128)} %bitcast.443, s32[]{:T(128)} %bitcast.444, ...), kind=kLoop, calls=%fused_computation.9.clone.1 | loop fusion | flops 696320 | bytes 98465 | tf_op jit(solution)/shard_map/jit(searchsorted)/jit(_searchsorted_scan_impl)/vmap(jit(_searchsorted_scan_impl))/while/body/eval_jaxpr/select_n | solution.py:83
  258.0 25.0 %fusion.141 = u32[8192]{0:T(1024)S(1)} fusion(u32[8192]{0:T(1024)S(1)} %get-tuple-element.525, u32[8192]{0:T(1024)S(1)} %get-tuple-element.524, s32[]{:T(128)} %bitcast.438, s32[]{:T(128)} %bitcast.439, s32[]{:T(128)} %bitcast.440, s32[]{:T(128)} %bitcast.441, s32[]{:T(128)} %bitcast.442, s32[]{:T(128)} %bitcast.443, s32[]{:T(128)} %bitcast.444, ...), kind=kLoop, calls=%fused_computation.8.clone.1 | loop fusion | flops 696320 | bytes 98465 | tf_op jit(solution)/shard_map/jit(searchsorted)/jit(_searchsorted_scan_impl)/vmap(jit(_searchsorted_scan_impl))/while/body/eval_jaxpr/select_n | solution.py:83
  283.0 25.0 %fusion.140 = u32[8192]{0:T(1024)S(1)} fusion(u32[8192]{0:T(1024)S(1)} %get-tuple-element.525, u32[8192]{0:T(1024)S(1)} %get-tuple-element.524, s32[]{:T(128)} %bitcast.438, s32[]{:T(128)} %bitcast.439, s32[]{:T(128)} %bitcast.440, s32[]{:T(128)} %bitcast.441, s32[]{:T(128)} %bitcast.442, s32[]{:T(128)} %bitcast.443, s32[]{:T(128)} %bitcast.444, ...), kind=kLoop, calls=%fused_computation.9.clone.1 | loop fusion | flops 696320 | bytes 98465 | tf_op jit(solution)/shard_map/jit(searchsorted)/jit(_searchsorted_scan_impl)/vmap(jit(_searchsorted_scan_impl))/while/body/eval_jaxpr/select_n | solution.py:83
  310.1 25.0 %fusion.141 = u32[8192]{0:T(1024)S(1)} fusion(u32[8192]{0:T(1024)S(1)} %get-tuple-element.525, u32[8192]{0:T(1024)S(1)} %get-tuple-element.524, s32[]{:T(128)} %bitcast.438, s32[]{:T(128)} %bitcast.439, s32[]{:T(128)} %bitcast.440, s32[]{:T(128)} %bitcast.441, s32[]{:T(128)} %bitcast.442, s32[]{:T(128)} %bitcast.443, s32[]{:T(128)} %bitcast.444, ...), kind=kLoop, calls=%fused_computation.8.clone.1 | loop fusion | flops 696320 | bytes 98465 | tf_op jit(solution)/shard_map/jit(searchsorted)/jit(_searchsorted_scan_impl)/vmap(jit(_searchsorted_scan_impl))/while/body/eval_jaxpr/select_n | solution.py:83
  335.1 25.0 %fusion.140 = u32[8192]{0:T(1024)S(1)} fusion(u32[8192]{0:T(1024)S(1)} %get-tuple-element.525, u32[8192]{0:T(1024)S(1)} %get-tuple-element.524, s32[]{:T(128)} %bitcast.438, s32[]{:T(128)} %bitcast.439, s32[]{:T(128)} %bitcast.440, s32[]{:T(128)} %bitcast.441, s32[]{:T(128)} %bitcast.442, s32[]{:T(128)} %bitcast.443, s32[]{:T(128)} %bitcast.444, ...), kind=kLoop, calls=%fused_computation.9.clone.1 | loop fusion | flops 696320 | bytes 98465 | tf_op jit(solution)/shard_map/jit(searchsorted)/jit(_searchsorted_scan_impl)/vmap(jit(_searchsorted_scan_impl))/while/body/eval_jaxpr/select_n | solution.py:83
  362.2 25.0 %fusion.141 = u32[8192]{0:T(1024)S(1)} fusion(u32[8192]{0:T(1024)S(1)} %get-tuple-element.525, u32[8192]{0:T(1024)S(1)} %get-tuple-element.524, s32[]{:T(128)} %bitcast.438, s32[]{:T(128)} %bitcast.439, s32[]{:T(128)} %bitcast.440, s32[]{:T(128)} %bitcast.441, s32[]{:T(128)} %bitcast.442, s32[]{:T(128)} %bitcast.443, s32[]{:T(128)} %bitcast.444, ...), kind=kLoop, calls=%fused_computation.8.clone.1 | loop fusion | flops 696320 | bytes 98465 | tf_op jit(solution)/shard_map/jit(searchsorted)/jit(_searchsorted_scan_impl)/vmap(jit(_searchsorted_scan_impl))/while/body/eval_jaxpr/select_n | solution.py:83
  387.2 25.0 %fusion.140 = u32[8192]{0:T(1024)S(1)} fusion(u32[8192]{0:T(1024)S(1)} %get-tuple-element.525, u32[8192]{0:T(1024)S(1)} %get-tuple-element.524, s32[]{:T(128)} %bitcast.438, s32[]{:T(128)} %bitcast.439, s32[]{:T(128)} %bitcast.440, s32[]{:T(128)} %bitcast.441, s32[]{:T(128)} %bitcast.442, s32[]{:T(128)} %bitcast.443, s32[]{:T(128)} %bitcast.444, ...), kind=kLoop, calls=%fused_computation.9.clone.1 | loop fusion | flops 696320 | bytes 98465 | tf_op jit(solution)/shard_map/jit(searchsorted)/jit(_searchsorted_scan_impl)/vmap(jit(_searchsorted_scan_impl))/while/body/eval_jaxpr/select_n | solution.py:83
  414.3 25.0 %fusion.141 = u32[8192]{0:T(1024)S(1)} fusion(u32[8192]{0:T(1024)S(1)} %get-tuple-element.525, u32[8192]{0:T(1024)S(1)} %get-tuple-element.524, s32[]{:T(128)} %bitcast.438, s32[]{:T(128)} %bitcast.439, s32[]{:T(128)} %bitcast.440, s32[]{:T(128)} %bitcast.441, s32[]{:T(128)} %bitcast.442, s32[]{:T(128)} %bitcast.443, s32[]{:T(128)} %bitcast.444, ...), kind=kLoop, calls=%fused_computation.8.clone.1 | loop fusion | flops 696320 | bytes 98465 | tf_op jit(solution)/shard_map/jit(searchsorted)/jit(_searchsorted_scan_impl)/vmap(jit(_searchsorted_scan_impl))/while/body/eval_jaxpr/select_n | solution.py:83
  439.2 25.0 %fusion.140 = u32[8192]{0:T(1024)S(1)} fusion(u32[8192]{0:T(1024)S(1)} %get-tuple-element.525, u32[8192]{0:T(1024)S(1)} %get-tuple-element.524, s32[]{:T(128)} %bitcast.438, s32[]{:T(128)} %bitcast.439, s32[]{:T(128)} %bitcast.440, s32[]{:T(128)} %bitcast.441, s32[]{:T(128)} %bitcast.442, s32[]{:T(128)} %bitcast.443, s32[]{:T(128)} %bitcast.444, ...), kind=kLoop, calls=%fused_computation.9.clone.1 | loop fusion | flops 696320 | bytes 98465 | tf_op jit(solution)/shard_map/jit(searchsorted)/jit(_searchsorted_scan_impl)/vmap(jit(_searchsorted_scan_impl))/while/body/eval_jaxpr/select_n | solution.py:83
  480.4 57.2 %scatter_custom_fusion = f32[40]{0:T(128)S(1)} fusion(s32[8192]{0:T(1024)} %convert_element_type.34, f32[8192]{0:T(1024)S(1)} %add_subtract_fusion.2, f32[]{:T(128)} %constant.148.clone.1), kind=kCustom, calls=%fused_computation.230 | custom fusion | flops 8192 | bytes 672 | tf_op jit(solution)/shard_map/scatter-add | solution.py:205
  539.7 25.7 %fusion.114 = (f32[8192]{0:T(1024)S(1)}, f32[8192]{0:T(1024)S(1)}, pred[8192]{0:T(1024)(128)(4,1)S(1)}, pred[8192]{0:T(1024)(128)(4,1)S(1)}, pred[8192]{0:T(1024...) fusion(f32[8192]{0:T(1024)S(1)} %bitcast.499, ...), kind=kLoop, calls=%fused_computation.235 | loop fusion | flops 712704 | bytes 458912 | tf_op jit(solution)/shard_map/mul | solution.py:214
  572.8 44.6 %all-reduce.7.cloned.1.call-done = f32[3,2048,16]{1,2,0:T(8,128)} async-done(((f32[3,2048,16]{1,2,0:T(8,128)}), f32[3,2048,16]{1,2,0:T(8,128)}) %all-reduce.7.cloned.1.call-update) | async-done | bytes 393232 | tf_op jit(solution)/shard_map/psum | solution.py:56
  618.9 25.8 %all_to_all.36 = f32[8,4,3,2048]{3,1,2,0:T(4,128)S(1)} all-to-all(f32[8,4,3,2048]{3,1,2,0:T(4,128)S(1)} %fusion.51), channel_id=1, replica_groups=mesh['det'=4,'obs'=8] {'obs'}, dimensions={0} | all-to-all | bytes 1572864 | tf_op jit(solution)/shard_map/all_to_all | solution.py:216
  648.0 23.4 %all_to_all.37 = f32[8,4,3,2048]{3,1,2,0:T(4,128)S(1)} all-to-all(f32[8,4,3,2048]{3,1,2,0:T(4,128)S(1)} %fusion.15), channel_id=1, replica_groups=mesh['det'=4,'obs'=8] {'obs'}, dimensions={0} | all-to-all | bytes 1572864 | tf_op jit(solution)/shard_map/all_to_all | solution.py:198
  685.9 57.2 %scatter_custom_fusion.1 = f32[40]{0:T(128)S(1)} fusion(s32[8192]{0:T(1024)} %convert_element_type.34, f32[8192]{0:T(1024)S(1)} %add_subtract_fusion.1, f32[]{:T(128)} %constant.148.clone.1), kind=kCustom, calls=%fused_computation.228 | custom fusion | flops 8192 | bytes 672 | tf_op jit(solution)/shard_map/scatter-add | solution.py:221
  743.7 37.6 %all-reduce = (f32[]{:T(128)}, f32[]{:T(128)}) all-reduce(f32[]{:T(128)} %get-tuple-element.196, f32[]{:T(128)} %get-tuple-element.195), channel_id=1, replica_groups=mesh['det'=4,'obs'=8] {'det','obs'}, use_global_device_ids=true, to_apply=%region_8.10 | all-reduce | flops 2 | bytes 16 | tf_op jit(solution)/shard_map/psum | solution.py:61
  783.2 42.2 %psum.53 = f32[]{:T(128)} all-reduce(f32[]{:T(128)} %get-tuple-element.209), channel_id=1, replica_groups=mesh['det'=4,'obs'=8] {'det','obs'}, use_global_device_ids=true, to_apply=%region_14.17 | all-reduce | flops 1 | bytes 8 | tf_op jit(solution)/shard_map/psum | solution.py:61
  828.9 25.8 %fusion.113 = (f32[8192]{0:T(1024)S(1)}, f32[8192]{0:T(1024)S(1)}) fusion(f32[8192]{0:T(1024)S(1)} %bitcast.501, pred[8192]{0:T(1024)(128)(4,1)} %get-tuple-element.252, pred[8192]{0:T(1024)(128)(4,1)} %get-tuple-element.251, pred[8192]{0:T(1024)(128)(4,1)} %get-tuple-element.250, pred[8192]{0:T(1024)(128)(4,1)} %get-tuple-element.249, ...), kind=kLoop, calls=%fused_computation.234 | loop fusion | flops 335872 | bytes 426144 | tf_op jit(solution)/shard_map/mul | solution.py:214
  862.0 43.5 %all-reduce.9.cloned.1.call-done = f32[3,2048,16]{1,2,0:T(8,128)} async-done(((f32[3,2048,16]{1,2,0:T(8,128)}), f32[3,2048,16]{1,2,0:T(8,128)}) %all-reduce.9.cloned.1.call-update) | async-done | bytes 393232 | tf_op jit(solution)/shard_map/psum | solution.py:56
  907.1 25.3 %all_to_all.38 = f32[8,4,3,2048]{3,1,2,0:T(4,128)S(1)} all-to-all(f32[8,4,3,2048]{3,1,2,0:T(4,128)S(1)} %fusion.49), channel_id=1, replica_groups=mesh['det'=4,'obs'=8] {'obs'}, dimensions={0} | all-to-all | bytes 1572864 | tf_op jit(solution)/shard_map/all_to_all | solution.py:216
  935.7 23.6 %all_to_all.39 = f32[8,4,3,2048]{3,1,2,0:T(4,128)S(1)} all-to-all(f32[8,4,3,2048]{3,1,2,0:T(4,128)S(1)} %fusion.13), channel_id=1, replica_groups=mesh['det'=4,'obs'=8] {'obs'}, dimensions={0} | all-to-all | bytes 1572864 | tf_op jit(solution)/shard_map/all_to_all | solution.py:198
  965.5 57.2 %scatter_custom_fusion.2 = f32[40]{0:T(128)S(1)} fusion(s32[8192]{0:T(1024)} %convert_element_type.34, f32[8192]{0:T(1024)S(1)} %add_subtract_fusion, f32[]{:T(128)} %constant.148.clone.1), kind=kCustom, calls=%fused_computation.226 | custom fusion | flops 8192 | bytes 672 | tf_op jit(solution)/shard_map/scatter-add | solution.py:221
  1023.2 37.6 %psum.55 = f32[]{:T(128)} all-reduce(f32[]{:T(128)} %multiply_reduce_fusion), channel_id=1, replica_groups=mesh['det'=4,'obs'=8] {'det','obs'}, use_global_device_ids=true, to_apply=%region_18.21 | all-reduce | flops 1 | bytes 8 | tf_op jit(solution)/shard_map/psum | solution.py:227
  (188 shorter events, 105.9 us)
Async XLA Ops:
  7.2 7.1 copy-start.14
  7.2 67.4 %all-reduce.5.cloned.1.call-start = ((), (), s32[]{:S(2)}) async-start(), calls=%async_computation.7 | async-start | bytes 2359296 | tf_op jit(solution)/shard_map/psum | solution.py:56
  8.9 5.3 copy-start
  8.9 5.3 copy-start.2
  11.0 3.3 copy-start.5
  16.2 1.1 copy-start.17
  17.5 453.4 %copy-start.7 = (s32[16]{0:T(128)}, s32[16]{0:T(128)S(1)}, u32[]{:S(2)}) copy-start(s32[16]{0:T(128)S(1)} %fusion.103) | copy-start | bytes 196
  18.3 60.7 %all-to-all-start = ((s32[8,1,4]{2,1,0:T(1,128)}), s32[8,1,4]{2,1,0:T(1,128)S(1)}, u32[]{:S(2)}, u32[]{:S(2)}) async-start(s32[8,1,4]{2,1,0:T(1,128)} %bitcast.10), calls=%async_computation | async-start | bytes 8192 | tf_op jit(solution)/shard_map/all_to_all | solution.py:181
  79.0 5.0 copy-start.15
  79.0 59.6 %all-to-all-start.1 = ((f32[8,4,9,2048]{3,1,2,0:T(4,128)}), f32[8,4,9,2048]{3,1,2,0:T(4,128)S(1)}, u32[]{:S(2)}, u32[]{:S(2)}) async-start(f32[8,4,9,2048]{3,1,2,0:T(4,128)} %fusion.34), calls=%async_computation.1 | async-start | bytes 4718592 | tf_op jit(solution)/shard_map/all_to_all | solution.py:180
  147.2 317.7 %all-to-all-start.2 = ((f32[8,4,3,2048]{3,1,2,0:T(4,128)}), f32[8,4,3,2048]{3,1,2,0:T(4,128)}, u32[]{:S(2)}, u32[]{:S(2)}) async-start(f32[8,4,3,2048]{3,1,2,0:T(4,128)} %fusion.17), calls=%async_computation.2 | async-start | bytes 1572864 | tf_op jit(solution)/shard_map/all_to_all | solution.py:198
  151.4 465.9 %all-reduce.7.cloned.1.call-start = ((), (), s32[]{:S(2)}) async-start(), calls=%async_computation.8 | async-start | bytes 786432 | tf_op jit(solution)/shard_map/psum | solution.py:56
  464.9 12.9 %copy-start.10 = (s32[1024]{0:T(1024)}, s32[1024]{0:T(1024)S(1)}, u32[]{:S(2)}) copy-start(s32[1024]{0:T(1024)S(1)} %pad_clamp_fusion) | copy-start | bytes 12292
  464.9 14.5 %copy-start.11 = (pred[32]{0:T(512)(128)(4,1)}, pred[32]{0:T(512)(128)(4,1)S(1)}, u32[]{:S(2)}) copy-start(pred[32]{0:T(512)(128)(4,1)S(1)} %compare_and_fusion.1) | copy-start | bytes 100
  473.8 5.8 copy-start.6
  473.8 6.6 copy-start.1
  473.8 6.6 copy-start.3
  473.8 6.6 copy-start.4
  572.7 332.8 %all-reduce.9.cloned.1.call-start = ((), (), s32[]{:S(2)}) async-start(), calls=%async_computation.9 | async-start | bytes 786432 | tf_op jit(solution)/shard_map/psum | solution.py:56
  672.0 4.3 copy-start.8
  679.2 5.7 copy-start.12
  959.9 1.1 copy-start.9
  962.6 1.9 copy-start.13
  962.6 99.6 %copy-start.16 = (s32[1,1,40]{2,1,0:T(1,128)S(1)}, s32[1,1,40]{2,1,0:T(1,128)}, u32[]{:S(2)}) copy-start(s32[1,1,40]{2,1,0:T(1,128)} %param.16) | copy-start | bytes 484
Sparse Core Ops, SparseCore 0:
  17.4 57.0 all-reduce.4
  572.8 44.4 all-reduce.6
  862.1 43.3 all-reduce.8
where the time goes:
time: 1080 us; the launch traced here: 1070 us
  other arithmetic  534 us (49%)
  blocking collectives  216 us (20%)
  waiting for transfers between devices  191 us (18%)
  local copies, waits for them, and re-layouts  58.7 us (5%)
  matrix products  35.6 us (3%)
  between operations  18.7 us (2%)
  starting transfers between devices  15.9 us (1%)
    select_n x12, other arithmetic, body(): jnp.searchsorted(ends, jnp.arange(samples, dtype=jnp.int32), side='right')  300 us
    psum x3, waiting for transfers between devices, combine_det(): total = lax.psum(partial_value, 'det')  138 us
    scatter-add x2, other arithmetic, body(): jax.ops.segment_sum(expanded - unbin_local(apply_local_map), base_index,...  114 us
    psum x2, blocking collectives, squares(): return lax.psum(jnp.sum(residual_vector * residual_vector), ('det', 'obs'))  79.9 us
    scatter-add x1, other arithmetic, body(): jax.ops.segment_sum(cleaned, base_index, num_segments=nbase, indices_are_...  57.2 us
    all_to_all x1, waiting for transfers between devices, body(): lax.all_to_all(pack_map(first_total), 'obs', split_axis=0, concat_axis=0,...  53.4 us
    mul x2, other arithmetic, body(): expanded * cos_w  51.5 us
    all_to_all x2, blocking collectives, body(): lax.all_to_all(pack_map(apply_total), 'obs', split_axis=0, concat_axis=0,...  51.2 us
  transfers between devices with their start and end apart: 6, of which 4 were waited for; matrix products, arithmetic and copies ran while one was open for 30% of the time, Pallas kernels for 0%

commit v1 on v0

v1 whole, which is shorter than its diff:
```python
import functools

import jax
import jax.numpy as jnp
from jax import lax
from jax.experimental import pallas as pl
from jax.experimental.pallas import tpu as pltpu
from jax.sharding import PartitionSpec as P

TILE = 256
BLK = 64
PATCH_PIX = 2048
LANES = 128
GROUP = 8
MESH = pl.DeviceIdType.MESH
F32 = jnp.float32
BF16 = jnp.bfloat16


def split3(x):
    hi = x.astype(BF16).astype(F32)
    rest = x - hi
    mid = rest.astype(BF16).astype(F32)
    return hi, mid, rest - mid


def eye(n):
    return lax.broadcasted_iota(jnp.int32, (n, n), 0) == lax.broadcasted_iota(jnp.int32, (n, n), 1)


def to_column(row):
    n = row.shape[1]
    return jnp.sum(jnp.where(eye(n), row, 0.0), axis=1, keepdims=True)


def to_row(col):
    n = col.shape[0]
    return jnp.sum(jnp.where(eye(n), col, 0.0), axis=0, keepdims=True)


def total(x):
    return jnp.sum(jnp.sum(x, axis=1, keepdims=True), axis=0, keepdims=True)


def kernel(
    ndet, nobs, tod_ref, angle_ref, pix_ref, tile_ref, len_ref, touched_ref,
    sol_ref, rate_ref,
    g_ref, equal_ref, inv_ref, ids_ref, ball1, ball2, ball3, ball4,
    a_send, a_recv, p_send, p_recv,
):
    n = ndet * nobs
    nchip = n // 2
    nbase = len_ref.shape[1]
    ntile = tile_ref.shape[1]
    patches = touched_ref.shape[1]
    blocks = PATCH_PIX // BLK
    me = lax.axis_index("det") * nobs + lax.axis_index("obs")
    chip = me // 2
    core = me % 2
    slot = core * nchip + chip
    other = 1 - core

    def place(c, k):
        flat = c * 2 + k
        return (flat // nobs, flat % nobs)

    barrier = pltpu.get_barrier_semaphore()

    def greet(r, carry):
        pl.semaphore_signal(
            barrier, inc=1, device_id=place((chip + r) % nchip, core), device_id_type=MESH
        )
        return carry

    lax.fori_loop(1, nchip, greet, 0)
    pl.semaphore_signal(barrier, inc=1, device_id=place(chip, other), device_id_type=MESH)

    def copy_a(ball, s, r, block, target):
        return pltpu.make_async_remote_copy(
            src_ref=ball.at[block], dst_ref=ball.at[block],
            send_sem=a_send.at[s], recv_sem=a_recv.at[s, r],
            device_id=target, device_id_type=MESH,
        )

    def copy_p(ball, s, block):
        return pltpu.make_async_remote_copy(
            src_ref=ball.at[block], dst_ref=ball.at[block],
            send_sem=p_send.at[s], recv_sem=p_recv.at[s],
            device_id=place(chip, other), device_id_type=MESH,
        )

    def start(ball, s):
        def one(r, carry):
            copy_a(ball, s, r, slot, place((chip + r) % nchip, core)).start()
            return carry

        lax.fori_loop(1, nchip, one, 0)
        copy_p(ball, s, slot).start()

    def finish(ball, s):
        def one(r, carry):
            came = core * nchip + (chip - r + nchip) % nchip
            copy_a(ball, s, r, came, place(chip, other)).wait_recv()
            copy_p(ball, s, came).start()
            return carry

        lax.fori_loop(1, nchip, one, 0)
        copy_a(ball, s, 1, pl.ds(0, nchip - 1), place(chip, other)).wait_send()
        copy_p(ball, s, pl.ds(core * nchip, nchip)).wait_send()
        copy_p(ball, s, pl.ds(other * nchip, nchip)).wait_recv()

    tile_row = tile_ref[...]
    patch_of = lax.shift_right_logical(tile_row, blocks.bit_length() - 1)
    block_of = jnp.bitwise_and(tile_row, blocks - 1).astype(F32)
    touched_col = to_column(touched_ref[...].astype(F32))
    chosen = lax.broadcasted_iota(jnp.int32, (patches, ntile), 0) == patch_of
    ids_row = (
        jnp.sum(jnp.where(chosen, touched_col, 0.0), axis=0, keepdims=True) * float(blocks)
        + block_of
    )
    ids_col = to_column(ids_row)
    id_rows = ids_ref.shape[1]
    spot = lax.broadcasted_iota(jnp.int32, (id_rows, LANES), 0) * LANES + lax.broadcasted_iota(
        jnp.int32, (id_rows, LANES), 1
    )
    mine = (spot >= slot * ntile) & (spot < slot * ntile + ntile)
    ids_wide = jnp.concatenate([ids_row] * (LANES // ntile), axis=1)
    ids_ref[slot] = jnp.where(mine, ids_wide, 0.0)

    len_row = len_ref[...].astype(F32)
    len_col = to_column(len_row)
    lower = lax.broadcasted_iota(jnp.int32, (nbase, nbase), 1) <= lax.broadcasted_iota(
        jnp.int32, (nbase, nbase), 0
    )
    ends_f = jnp.sum(jnp.where(lower, len_row, 0.0), axis=1, keepdims=True)
    ends = ends_f.astype(jnp.int32)
    starts = (ends_f - len_col).astype(jnp.int32)

    pl.semaphore_wait(barrier, nchip)
    start(ids_ref, 2)

    pixel = lax.broadcasted_iota(jnp.int32, (BLK, TILE), 0)
    where_in = lax.broadcasted_iota(jnp.int32, (1, TILE), 1)
    per = TILE // LANES

    def build(g, acc):
        at = pl.multiple_of(g * GROUP * per, GROUP * per)
        tod = tod_ref[pl.ds(at, GROUP * per), :]
        angle = angle_ref[pl.ds(at, GROUP * per), :]
        pix = pix_ref[pl.ds(at, GROUP * per), :]
        cw = jnp.cos(2.0 * angle)
        sw = jnp.sin(2.0 * angle)
        c3 = split3(cw)
        s3 = split3(sw)
        parts = [split3(v) for v in (tod, tod * cw, tod * sw, cw * cw, cw * sw)]
        rows = []

        def line(x, i):
            return jnp.concatenate([x[per * i + j : per * i + j + 1] for j in range(per)], axis=1)

        for i in range(GROUP):
            pos = where_in + (g * GROUP + i) * TILE
            ind = (pos >= starts) & (pos < ends)
            tod_line = line(tod, i)
            acc = acc + jnp.where(ind, tod_line, 0.0)
            oh = line(pix, i) == pixel
            pieces = []
            for j in range(3):
                pieces.append(jnp.where(oh, line(c3[j], i), 0.0))
                pieces.append(jnp.where(oh, line(s3[j], i), 0.0))
            pieces.append(jnp.where(oh, 1.0, 0.0))
            rhs = jnp.concatenate(pieces, axis=0).astype(BF16)
            vals = [line(p[j], i) for j in range(3) for p in parts]
            vals.append(jnp.zeros((1, TILE), F32))
            lhs = jnp.concatenate([jnp.where(ind, 1.0, 0.0)] + vals, axis=0).astype(BF16)
            res = lax.dot_general(
                lhs, rhs, (((1,), (1,)), ((), ())), preferred_element_type=F32
            )
            top = res[:nbase]
            cs = top[:, 0:128] + top[:, 128:256] + top[:, 256:384]
            one = jnp.concatenate([top[:, 384:448], jnp.zeros((nbase, BLK), F32)], axis=1)
            gt = jnp.concatenate([cs, one], axis=1)
            g_ref[g * GROUP + i] = gt
            hit = jnp.sum(gt, axis=0, keepdims=True)
            v = res[nbase:, 384:448]
            v = v[0:5] + v[5:10] + v[10:15]
            rows.append(
                jnp.concatenate(
                    [v[1:2], v[2:3], v[0:1], hit[:, 128:192], hit[:, 0:128], v[3:4], v[4:5]],
                    axis=1,
                )
            )
        ball1[slot, pl.ds(pl.multiple_of(g * GROUP, GROUP), GROUP), :] = jnp.concatenate(
            rows, axis=0
        )
        return acc

    acc = lax.fori_loop(0, ntile // GROUP, build, jnp.zeros((nbase, TILE), F32))
    f_tod = jnp.sum(acc, axis=1, keepdims=True)

    start(ball1, 1)
    finish(ids_ref, 2)
    id_table = lax.fori_loop(
        0, n, lambda j, t: t + ids_ref[j], jnp.zeros((id_rows, LANES), F32)
    )
    for q in range(id_rows):
        equal_ref[:, q * LANES : (q + 1) * LANES] = jnp.where(
            ids_col == id_table[q : q + 1, :], 1.0, 0.0
        ).astype(BF16)
    finish(ball1, 1)

    step = TILE // ntile

    def match(ball):
        width = ball.shape[2]

        def one(j, s):
            b = ball[pl.ds(j * step, step)].reshape(TILE, width)
            hi = b.astype(BF16)
            rest = b - hi.astype(F32)
            mid = rest.astype(BF16)
            lo = (rest - mid.astype(F32)).astype(BF16)
            e = equal_ref[:, pl.ds(pl.multiple_of(j * TILE, TILE), TILE)]
            for part in (hi, mid, lo):
                s = s + jnp.dot(e, part, preferred_element_type=F32)
            return s

        return lax.fori_loop(0, n // step, one, jnp.zeros((ntile, width), F32))

    def solve(tc, ts, t):
        m1 = inv_ref[0] * t + inv_ref[1] * tc + inv_ref[2] * ts
        m2 = inv_ref[1] * t + inv_ref[3] * tc + inv_ref[4] * ts
        m3 = inv_ref[2] * t + inv_ref[4] * tc + inv_ref[5] * ts
        return jnp.concatenate([m2, m3, m1, jnp.zeros_like(m1)], axis=1)

    def unbin(m):
        out = jnp.zeros((nbase, 4 * BLK), F32)
        for t in range(ntile):
            out = out + g_ref[t] * m[t : t + 1, :]
        return jnp.sum(out, axis=1, keepdims=True)

    def bin_out(ball, d, scalar):
        pad = lax.broadcasted_iota(jnp.int32, (GROUP, 4 * BLK), 1) >= 3 * BLK
        for g in range(ntile // GROUP):
            rows = [
                jnp.sum(g_ref[g * GROUP + i] * d, axis=0, keepdims=True) for i in range(GROUP)
            ]
            ball[slot, g * GROUP : (g + 1) * GROUP, :] = jnp.where(
                pad, scalar, jnp.concatenate(rows, axis=0)
            )

    def scalar_of(ball):
        s = lax.fori_loop(
            0, n, lambda j, t: t + ball[j, 0:8, 128:256], jnp.zeros((8, LANES), F32)
        )
        return s[0:1, BLK : BLK + 1]

    def apply(ball, d):
        s = match(ball)
        return len_col * d - unbin(solve(s[:, 0:64], s[:, 64:128], s[:, 128:192]))

    s1 = match(ball1)
    a11 = s1[:, 192:256] + 1.0
    a12 = s1[:, 256:320]
    a13 = s1[:, 320:384]
    a22 = s1[:, 384:448] + 1.0
    a23 = s1[:, 448:512]
    a33 = (s1[:, 192:256] - s1[:, 384:448]) + 1.0
    c11 = a22 * a33 - a23 * a23
    c12 = a13 * a23 - a12 * a33
    c13 = a12 * a23 - a13 * a22
    c22 = a11 * a33 - a13 * a13
    c23 = a12 * a13 - a11 * a23
    c33 = a11 * a22 - a12 * a12
    determinant = a11 * c11 + a12 * c12 + a13 * c13
    for i, c in enumerate((c11, c12, c13, c22, c23, c33)):
        inv_ref[i] = c / determinant
    r0 = f_tod - unbin(solve(s1[:, 0:64], s1[:, 64:128], s1[:, 128:192]))

    bin_out(ball2, r0, total(r0 * r0))
    start(ball2, 0)
    finish(ball2, 0)
    rr0 = scalar_of(ball2)
    q0 = apply(ball2, r0)

    bin_out(ball3, q0, total(r0 * q0))
    start(ball3, 1)
    finish(ball3, 1)
    rq = scalar_of(ball3)
    w = apply(ball3, q0)
    alpha0 = rr0 / rq
    r1 = r0 - alpha0 * q0
    z = q0 - alpha0 * w

    lane = lax.broadcasted_iota(jnp.int32, (8, LANES), 1)
    sums = (total(r1 * r1), total(r1 * z), total(r1 * q0) + total(r0 * z))
    packed = jnp.zeros((8, LANES), F32)
    for i, v in enumerate(sums):
        packed = jnp.where(lane == i, v, packed)
    ball4[slot] = packed
    start(ball4, 0)
    finish(ball4, 0)
    got = lax.fori_loop(0, n, lambda j, t: t + ball4[j], jnp.zeros((8, LANES), F32))
    rr1 = got[0:1, 0:1]
    beta = rr1 / rr0
    d1 = r1 + beta * r0
    image = z + beta * q0
    curve = got[0:1, 1:2] + beta * got[0:1, 2:3] + beta * beta * rq
    alpha1 = rr1 / curve
    sol_ref[...] = to_row(alpha0 * r0 + alpha1 * d1)
    rate_ref[...] = to_row((r1 - alpha1 * image) / len_col)


def solution(mesh):
    ndet = mesh.shape["det"]
    nobs = mesh.shape["obs"]
    n = ndet * nobs

    def body(tod, angle, pix_in, tile_block, base_len, touched):
        samples = tod.shape[2]
        ntile = tile_block.shape[2]
        nbase = base_len.shape[2]
        id_rows = n * ntile // LANES
        vmem = pl.BlockSpec(memory_space=pltpu.VMEM)
        sol, rate = pl.pallas_call(
            functools.partial(kernel, ndet, nobs),
            out_shape=[jax.ShapeDtypeStruct((1, nbase), F32)] * 2,
            in_specs=[vmem] * 6,
            out_specs=[vmem] * 2,
            scratch_shapes=[
                pltpu.VMEM((ntile, nbase, 4 * BLK), F32),
                pltpu.VMEM((ntile, n * ntile), BF16),
                pltpu.VMEM((6, ntile, BLK), F32),
                pltpu.VMEM((n, id_rows, LANES), F32),
                pltpu.VMEM((n, ntile, 8 * BLK), F32),
                pltpu.VMEM((n, ntile, 4 * BLK), F32),
                pltpu.VMEM((n, ntile, 4 * BLK), F32),
                pltpu.VMEM((n, 8, LANES), F32),
                pltpu.SemaphoreType.DMA((3,)),
                pltpu.SemaphoreType.DMA((3, n // 2)),
                pltpu.SemaphoreType.DMA((3,)),
                pltpu.SemaphoreType.DMA((3,)),
            ],
            compiler_params=pltpu.CompilerParams(
                collective_id=0, has_side_effects=True, vmem_limit_bytes=60 * 1024 * 1024
            ),
        )(
            tod.reshape(samples // LANES, LANES),
            angle.reshape(samples // LANES, LANES),
            pix_in.reshape(samples // LANES, LANES),
            tile_block.reshape(1, ntile),
            base_len.reshape(1, nbase),
            touched,
        )
        return sol.reshape(1, 1, nbase), rate.reshape(1, 1, nbase)

    spec = P("det", "obs", None)
    return jax.shard_map(
        body,
        mesh=mesh,
        in_specs=(spec, spec, spec, spec, spec, P("obs", None)),
        out_specs=(spec, spec),
        check_vma=False,
    )
```

time: 1080 us -> 79.3 us (0.07)
  other arithmetic: 534 us -> 0 us
  blocking collectives: 216 us -> 0 us
  waiting for transfers between devices: 191 us -> 0 us
  Pallas kernels: 0 us -> 76.6 us
  local copies, waits for them, and re-layouts: 58.7 us -> 1.8 us
  matrix products: 35.6 us -> 0 us
  between operations: 18.7 us -> 0.65 us
  starting transfers between devices: 15.9 us -> 0 us
    select_n x17 -> x0, other arithmetic: 300 us -> none  [the longest x12 300 us: body(): jnp.searchsorted(ends, jnp.arange(samples, dtype=jnp.int32), side='right')]
    scatter-add x3 -> x0, other arithmetic: 172 us -> none  [the longest x2 114 us: body(): jax.ops.segment_sum(expanded - unbin_local(apply_local_map), base_index,...]
    psum x3 -> x0, waiting for transfers between devices: 138 us -> none  [combine_det(): total = lax.psum(partial_value, 'det')]
    psum x3 -> x0, blocking collectives: 117 us -> none  [the longest x2 79.9 us: squares(): return lax.psum(jnp.sum(residual_vector * residual_vector), ('det', 'obs'))]
    all_to_all x4 -> x0, blocking collectives: 98.1 us -> none  [the longest x2 51.2 us: body(): lax.all_to_all(pack_map(apply_total), 'obs', split_axis=0, concat_axis=0,...]
    pallas_call x0 -> x1, Pallas kernels: none -> 76.6 us  [body(): pl.pallas_call(functools.partial(kernel, ndet, nobs), out_shape=[jax.Shap...]
    all_to_all x3 -> x0, waiting for transfers between devices: 53.4 us -> none  [the longest x1 53.4 us: body(): lax.all_to_all(pack_map(first_total), 'obs', split_axis=0, concat_axis=0,...]
    mul x5 -> x0, other arithmetic: 52.3 us -> none  [the longest x2 51.5 us: body(): expanded * cos_w]
  transfers between devices with their start and end apart: 6 -> 0, of which waited for: 4 -> 0; matrix products, arithmetic and copies ran while one was open for 30% -> 0% of each run, Pallas kernels for 0% -> 0%
where the time goes in v1:
time: 79.3 us; the launch traced here: 79.1 us
  Pallas kernels  76.6 us (97%)
  local copies, waits for them, and re-layouts  1.8 us (2%)
    pallas_call x1, Pallas kernels, body(): pl.pallas_call(functools.partial(kernel, ndet, nobs), out_shape=[jax.Shap...  76.6 us
    unnamed x6, local copies, waits for them, and re-layouts  1.8 us

profile of v1, /device:TPU:0, one launch (start us, length us, event | category | flops | bytes accessed | tf_op | source)
XLA Modules:
  0.0 79.1 jit_solution(15942269283191966294)
XLA Ops:
  0.6 76.6 %shard_map.77 = (f32[1,40]{1,0:T(1,128)}, f32[1,40]{1,0:T(1,128)}) custom-call(f32[64,128]{1,0:T(8,128)} %bitcast.7, f32[64,128]{1,0:T(8,128)} %bitcast.8, s32[64,128]{1,0:T(8,128)} %bitcast.9, s32[1,32]{1,0:T(1,128)} %bitcast.10, s32[1,40]{1,0:T(1,128)} %bitcast.11, s32[1,16]{1,0:T(1,128)} %touched_ref.1), custom_call_target="tpu_custom_call" | custom-call | tf_op jit(solution)/shard_map/pallas_call | solution.py:325
  77.3 0.0 copy-start.1
  77.3 0.7 copy-done.1
  77.9 0.0 copy-start
  77.9 0.5 copy.10
  78.5 0.1 copy-done
  78.6 0.5 copy.11
Async XLA Ops:
  77.3 0.7 copy-start.1
  77.9 0.6 copy-start

commit v2 on v1

--- a/solution.py
+++ b/solution.py
@@ -44,9 +44,9 @@
 
 def kernel(
     ndet, nobs, tod_ref, angle_ref, pix_ref, tile_ref, len_ref, touched_ref,
-    sol_ref, rate_ref,
+    out_ref,
     g_ref, equal_ref, inv_ref, ids_ref, ball1, ball2, ball3, ball4,
-    a_send, a_recv, p_send, p_recv,
+    a_send, a_recv, p_send, p_recv, d_send, d_recv,
 ):
     n = ndet * nobs
     nchip = n // 2
@@ -67,47 +67,91 @@
     barrier = pltpu.get_barrier_semaphore()
 
     def greet(r, carry):
+        flat = (me + r) % n
         pl.semaphore_signal(
-            barrier, inc=1, device_id=place((chip + r) % nchip, core), device_id_type=MESH
+            barrier, inc=1, device_id=(flat // nobs, flat % nobs), device_id_type=MESH
         )
         return carry
 
-    lax.fori_loop(1, nchip, greet, 0)
-    pl.semaphore_signal(barrier, inc=1, device_id=place(chip, other), device_id_type=MESH)
-
-    def copy_a(ball, s, r, block, target):
+    lax.fori_loop(1, n, greet, 0)
+
+    def copy(ball, block, send, recv, target):
         return pltpu.make_async_remote_copy(
             src_ref=ball.at[block], dst_ref=ball.at[block],
-            send_sem=a_send.at[s], recv_sem=a_recv.at[s, r],
-            device_id=target, device_id_type=MESH,
-        )
-
-    def copy_p(ball, s, block):
-        return pltpu.make_async_remote_copy(
-            src_ref=ball.at[block], dst_ref=ball.at[block],
-            send_sem=p_send.at[s], recv_sem=p_recv.at[s],
-            device_id=place(chip, other), device_id_type=MESH,
-        )
+            send_sem=send, recv_sem=recv, device_id=target, device_id_type=MESH,
+        )
+
+    def start_direct(ball, s):
+        def one(r, carry):
+            flat = (me + r) % n
+            target = (flat // nobs, flat % nobs)
+            copy(ball, slot, d_send.at[s], d_recv.at[s], target).start()
+            return carry
+
+        lax.fori_loop(1, n, one, 0)
+
+    def finish_direct(ball, s):
+        copy(ball, pl.ds(0, n - 1), d_send.at[s], d_recv.at[s], place(chip, other)).wait()
+
+    det = lax.axis_index("det")
+    line = nobs // 2
+    spot_z = chip % line
+    near = (det + 1 - 2 * (det % 2), (det + 2) % ndet)
+    diagonal = (near[0] + 2) % ndet
+
+    def of(d, r):
+        return core * nchip + d * line + (spot_z - r + line) % line
+
+    def to_near(k):
+        return (near[k], spot_z * 2 + core)
+
+    def partner(ball, s, block):
+        return copy(ball, block, p_send.at[s], p_recv.at[s], place(chip, other))
+
+    def share(ball, s, r):
+        for k in range(2):
+            copy(ball, of(det, r), a_send.at[s], a_recv.at[s, 1 + k, r], to_near(k)).start()
+        partner(ball, s, of(det, r)).start()
 
     def start(ball, s):
-        def one(r, carry):
-            copy_a(ball, s, r, slot, place((chip + r) % nchip, core)).start()
-            return carry
-
-        lax.fori_loop(1, nchip, one, 0)
-        copy_p(ball, s, slot).start()
+        for r in range(1, line):
+            target = (det, ((spot_z + r) % line) * 2 + core)
+            copy(ball, slot, a_send.at[s], a_recv.at[s, 0, r], target).start()
+        share(ball, s, 0)
+
+    def relay(ball, s, r):
+        half = ball.shape[1] // 2
+        for k in range(2):
+            block = of(near[k], r)
+            copy(ball, block, a_send.at[s], a_recv.at[s, 1 + k, r], to_near(k)).wait_recv()
+            piece = ball.at[block, pl.ds(k * half, half)]
+            pltpu.make_async_remote_copy(
+                src_ref=piece, dst_ref=piece,
+                send_sem=a_send.at[s], recv_sem=a_recv.at[s, 3, r],
+                device_id=to_near(1 - k), device_id_type=MESH,
+            ).start()
+            partner(ball, s, block).start()
+
+    def last(ball, s, r):
+        block = of(diagonal, r)
+        copy(ball, block, a_send.at[s], a_recv.at[s, 3, r], place(chip, other)).wait_recv()
+        partner(ball, s, block).start()
 
     def finish(ball, s):
-        def one(r, carry):
-            came = core * nchip + (chip - r + nchip) % nchip
-            copy_a(ball, s, r, came, place(chip, other)).wait_recv()
-            copy_p(ball, s, came).start()
-            return carry
-
-        lax.fori_loop(1, nchip, one, 0)
-        copy_a(ball, s, 1, pl.ds(0, nchip - 1), place(chip, other)).wait_send()
-        copy_p(ball, s, pl.ds(core * nchip, nchip)).wait_send()
-        copy_p(ball, s, pl.ds(other * nchip, nchip)).wait_recv()
+        for r in range(line + 2):
+            if 0 < r < line:
+                copy(
+                    ball, of(det, r), a_send.at[s], a_recv.at[s, 0, r], place(chip, other)
+                ).wait_recv()
+                share(ball, s, r)
+            if 1 <= r <= line:
+                relay(ball, s, r - 1)
+            if 2 <= r:
+                last(ball, s, r - 2)
+        everyone = place(chip, other)
+        copy(ball, pl.ds(0, nchip - 1), a_send.at[s], p_recv.at[s], everyone).wait_send()
+        partner(ball, s, pl.ds(core * nchip, nchip)).wait_send()
+        partner(ball, s, pl.ds(other * nchip, nchip)).wait_recv()
 
     tile_row = tile_ref[...]
     patch_of = lax.shift_right_logical(tile_row, blocks.bit_length() - 1)
@@ -119,13 +163,11 @@
         + block_of
     )
     ids_col = to_column(ids_row)
-    id_rows = ids_ref.shape[1]
-    spot = lax.broadcasted_iota(jnp.int32, (id_rows, LANES), 0) * LANES + lax.broadcasted_iota(
-        jnp.int32, (id_rows, LANES), 1
-    )
-    mine = (spot >= slot * ntile) & (spot < slot * ntile + ntile)
-    ids_wide = jnp.concatenate([ids_row] * (LANES // ntile), axis=1)
-    ids_ref[slot] = jnp.where(mine, ids_wide, 0.0)
+    per_row = LANES // ntile
+    id_rows = n // per_row
+    lane_row = lax.broadcasted_iota(jnp.int32, (1, LANES), 1) - (slot % per_row) * ntile
+    mine = (lane_row >= 0) & (lane_row < ntile)
+    ids_ref[slot] = jnp.where(mine, jnp.concatenate([ids_row] * per_row, axis=1), 0.0)
 
     len_row = len_ref[...].astype(F32)
     len_col = to_column(len_row)
@@ -136,8 +178,8 @@
     ends = ends_f.astype(jnp.int32)
     starts = (ends_f - len_col).astype(jnp.int32)
 
-    pl.semaphore_wait(barrier, nchip)
-    start(ids_ref, 2)
+    pl.semaphore_wait(barrier, n - 1)
+    start_direct(ids_ref, 0)
 
     pixel = lax.broadcasted_iota(jnp.int32, (BLK, TILE), 0)
     where_in = lax.broadcasted_iota(jnp.int32, (1, TILE), 1)
@@ -155,22 +197,22 @@
         parts = [split3(v) for v in (tod, tod * cw, tod * sw, cw * cw, cw * sw)]
         rows = []
 
-        def line(x, i):
+        def strip(x, i):
             return jnp.concatenate([x[per * i + j : per * i + j + 1] for j in range(per)], axis=1)
 
         for i in range(GROUP):
             pos = where_in + (g * GROUP + i) * TILE
             ind = (pos >= starts) & (pos < ends)
-            tod_line = line(tod, i)
+            tod_line = strip(tod, i)
             acc = acc + jnp.where(ind, tod_line, 0.0)
-            oh = line(pix, i) == pixel
+            oh = strip(pix, i) == pixel
             pieces = []
             for j in range(3):
-                pieces.append(jnp.where(oh, line(c3[j], i), 0.0))
-                pieces.append(jnp.where(oh, line(s3[j], i), 0.0))
+                pieces.append(jnp.where(oh, strip(c3[j], i), 0.0))
+                pieces.append(jnp.where(oh, strip(s3[j], i), 0.0))
             pieces.append(jnp.where(oh, 1.0, 0.0))
             rhs = jnp.concatenate(pieces, axis=0).astype(BF16)
-            vals = [line(p[j], i) for j in range(3) for p in parts]
+            vals = [strip(p[j], i) for j in range(3) for p in parts]
             vals.append(jnp.zeros((1, TILE), F32))
             lhs = jnp.concatenate([jnp.where(ind, 1.0, 0.0)] + vals, axis=0).astype(BF16)
             res = lax.dot_general(
@@ -199,14 +241,12 @@
     f_tod = jnp.sum(acc, axis=1, keepdims=True)
 
     start(ball1, 1)
-    finish(ids_ref, 2)
-    id_table = lax.fori_loop(
-        0, n, lambda j, t: t + ids_ref[j], jnp.zeros((id_rows, LANES), F32)
-    )
+    finish_direct(ids_ref, 0)
     for q in range(id_rows):
-        equal_ref[:, q * LANES : (q + 1) * LANES] = jnp.where(
-            ids_col == id_table[q : q + 1, :], 1.0, 0.0
-        ).astype(BF16)
+        ids_q = sum(ids_ref[q * per_row + j] for j in range(per_row))
+        equal_ref[:, q * LANES : (q + 1) * LANES] = jnp.where(ids_col == ids_q, 1.0, 0.0).astype(
+            BF16
+        )
     finish(ball1, 1)
 
     step = TILE // ntile
@@ -292,23 +332,23 @@
     r1 = r0 - alpha0 * q0
     z = q0 - alpha0 * w
 
-    lane = lax.broadcasted_iota(jnp.int32, (8, LANES), 1)
+    lane = lax.broadcasted_iota(jnp.int32, (1, LANES), 1)
     sums = (total(r1 * r1), total(r1 * z), total(r1 * q0) + total(r0 * z))
-    packed = jnp.zeros((8, LANES), F32)
+    packed = jnp.zeros((1, LANES), F32)
     for i, v in enumerate(sums):
         packed = jnp.where(lane == i, v, packed)
     ball4[slot] = packed
-    start(ball4, 0)
-    finish(ball4, 0)
-    got = lax.fori_loop(0, n, lambda j, t: t + ball4[j], jnp.zeros((8, LANES), F32))
+    start_direct(ball4, 1)
+    finish_direct(ball4, 1)
+    got = lax.fori_loop(0, n, lambda j, t: t + ball4[j], jnp.zeros((1, LANES), F32))
     rr1 = got[0:1, 0:1]
     beta = rr1 / rr0
     d1 = r1 + beta * r0
     image = z + beta * q0
     curve = got[0:1, 1:2] + beta * got[0:1, 2:3] + beta * beta * rq
     alpha1 = rr1 / curve
-    sol_ref[...] = to_row(alpha0 * r0 + alpha1 * d1)
-    rate_ref[...] = to_row((r1 - alpha1 * image) / len_col)
+    out_ref[0:1, :] = to_row(alpha0 * r0 + alpha1 * d1)
+    out_ref[1:2, :] = to_row((r1 - alpha1 * image) / len_col)
 
 
 def solution(mesh):
@@ -320,26 +360,27 @@
         samples = tod.shape[2]
         ntile = tile_block.shape[2]
         nbase = base_len.shape[2]
-        id_rows = n * ntile // LANES
         vmem = pl.BlockSpec(memory_space=pltpu.VMEM)
-        sol, rate = pl.pallas_call(
+        out = pl.pallas_call(
             functools.partial(kernel, ndet, nobs),
-            out_shape=[jax.ShapeDtypeStruct((1, nbase), F32)] * 2,
+            out_shape=jax.ShapeDtypeStruct((2, nbase), F32),
             in_specs=[vmem] * 6,
-            out_specs=[vmem] * 2,
+            out_specs=vmem,
             scratch_shapes=[
                 pltpu.VMEM((ntile, nbase, 4 * BLK), F32),
                 pltpu.VMEM((ntile, n * ntile), BF16),
                 pltpu.VMEM((6, ntile, BLK), F32),
-                pltpu.VMEM((n, id_rows, LANES), F32),
+                pltpu.VMEM((n, 1, LANES), F32),
                 pltpu.VMEM((n, ntile, 8 * BLK), F32),
                 pltpu.VMEM((n, ntile, 4 * BLK), F32),
                 pltpu.VMEM((n, ntile, 4 * BLK), F32),
-                pltpu.VMEM((n, 8, LANES), F32),
-                pltpu.SemaphoreType.DMA((3,)),
-                pltpu.SemaphoreType.DMA((3, n // 2)),
-                pltpu.SemaphoreType.DMA((3,)),
-                pltpu.SemaphoreType.DMA((3,)),
+                pltpu.VMEM((n, 1, LANES), F32),
+                pltpu.SemaphoreType.DMA((2,)),
+                pltpu.SemaphoreType.DMA((2, 4, nobs // 2)),
+                pltpu.SemaphoreType.DMA((2,)),
+                pltpu.SemaphoreType.DMA((2,)),
+                pltpu.SemaphoreType.DMA((2,)),
+                pltpu.SemaphoreType.DMA((2,)),
             ],
             compiler_params=pltpu.CompilerParams(
                 collective_id=0, has_side_effects=True, vmem_limit_bytes=60 * 1024 * 1024
@@ -352,7 +393,7 @@
             base_len.reshape(1, nbase),
             touched,
         )
-        return sol.reshape(1, 1, nbase), rate.reshape(1, 1, nbase)
+        return out[0].reshape(1, 1, nbase), out[1].reshape(1, 1, nbase)
 
     spec = P("det", "obs", None)
     return jax.shard_map(

time: 79.3 us -> 66.3 us (0.84)
  Pallas kernels: 76.6 us -> 64.2 us
    pallas_call x1, Pallas kernels: 76.6 us -> 64.2 us  [body(): pl.pallas_call(functools.partial(kernel, ndet, nobs), out_shape=jax.Shape...]
    unnamed x6 -> x0, local copies, waits for them, and re-layouts: 1.8 us -> none
    another operation x0 -> x1, local copies, waits for them, and re-layouts: none -> 1.25 us  [body(): return (out[0].reshape(1, 1, nbase), out[1].reshape(1, 1, nbase))]
where the time goes in v2:
time: 66.3 us; the launch traced here: 66.1 us
  Pallas kernels  64.2 us (97%)
  local copies, waits for them, and re-layouts  1.25 us (2%)
    pallas_call x1, Pallas kernels, body(): pl.pallas_call(functools.partial(kernel, ndet, nobs), out_shape=jax.Shape...  64.2 us

profile of v2, /device:TPU:0, one launch (start us, length us, event | category | flops | bytes accessed | tf_op | source)
XLA Modules:
  0.0 66.1 jit_solution(8373217513879164997)
XLA Ops:
  0.6 64.2 %shard_map.77 = f32[2,40]{1,0:T(2,128)} custom-call(f32[64,128]{1,0:T(8,128)} %bitcast.9, f32[64,128]{1,0:T(8,128)} %bitcast.10, s32[64,128]{1,0:T(8,128)} %bitcast.11, s32[1,32]{1,0:T(1,128)} %bitcast.12, s32[1,40]{1,0:T(1,128)} %bitcast.13, s32[1,16]{1,0:T(1,128)} %touched_ref.1), custom_call_target="tpu_custom_call" | custom-call | tf_op jit(solution)/shard_map/pallas_call | solution.py:364
  64.8 1.3 %slice_bitcast_fusion = (f32[1,1,40]{2,1,0:T(1,128)}, f32[1,1,40]{2,1,0:T(1,128)}) fusion(f32[2,40]{1,0:T(2,128)} %shard_map.77), kind=kLoop, calls=%fused_computation | loop fusion | bytes 640 | tf_op jit(solution)/shard_map/reshape;squeeze | solution.py:396

commit v3 on v2

--- a/solution.py
+++ b/solution.py
@@ -45,7 +45,7 @@
 def kernel(
     ndet, nobs, tod_ref, angle_ref, pix_ref, tile_ref, len_ref, touched_ref,
     out_ref,
-    g_ref, equal_ref, inv_ref, ids_ref, ball1, ball2, ball3, ball4,
+    g_ref, equal_ref, inv_ref, ids_ref, ball1, ball2, ball3, ball4, sums2, sums3,
     a_send, a_recv, p_send, p_recv, d_send, d_recv,
 ):
     n = ndet * nobs
@@ -254,8 +254,19 @@
     def match(ball):
         width = ball.shape[2]
 
+        packed = width == 2 * BLK
+        width = 3 * BLK if packed else width
+
         def one(j, s):
-            b = ball[pl.ds(j * step, step)].reshape(TILE, width)
+            b = ball[pl.ds(j * step, step)]
+            if packed:
+                ones = b[:, ntile:]
+                ones = jnp.concatenate([ones[:, :, :BLK], ones[:, :, BLK:]], axis=1)
+                b = jnp.concatenate(
+                    [b[:, :ntile].reshape(TILE, 2 * BLK), ones.reshape(TILE, BLK)], axis=1
+                )
+            else:
+                b = b.reshape(TILE, width)
             hi = b.astype(BF16)
             rest = b - hi.astype(F32)
             mid = rest.astype(BF16)
@@ -279,21 +290,24 @@
             out = out + g_ref[t] * m[t : t + 1, :]
         return jnp.sum(out, axis=1, keepdims=True)
 
-    def bin_out(ball, d, scalar):
-        pad = lax.broadcasted_iota(jnp.int32, (GROUP, 4 * BLK), 1) >= 3 * BLK
+    def bin_out(ball, scalars, d, scalar):
+        scalars[slot] = jnp.broadcast_to(scalar, (1, LANES))
+        ones = []
         for g in range(ntile // GROUP):
-            rows = [
-                jnp.sum(g_ref[g * GROUP + i] * d, axis=0, keepdims=True) for i in range(GROUP)
-            ]
-            ball[slot, g * GROUP : (g + 1) * GROUP, :] = jnp.where(
-                pad, scalar, jnp.concatenate(rows, axis=0)
+            rows = jnp.concatenate(
+                [jnp.sum(g_ref[g * GROUP + i] * d, axis=0, keepdims=True) for i in range(GROUP)],
+                axis=0,
             )
-
-    def scalar_of(ball):
-        s = lax.fori_loop(
-            0, n, lambda j, t: t + ball[j, 0:8, 128:256], jnp.zeros((8, LANES), F32)
-        )
-        return s[0:1, BLK : BLK + 1]
+            ball[slot, g * GROUP : (g + 1) * GROUP, :] = rows[:, : 2 * BLK]
+            ones.append(rows[:, 2 * BLK : 3 * BLK])
+        pairs = len(ones) // 2
+        for g in range(pairs):
+            ball[slot, ntile + g * GROUP : ntile + (g + 1) * GROUP, :] = jnp.concatenate(
+                [ones[g], ones[g + pairs]], axis=1
+            )
+
+    def gathered(ball):
+        return lax.fori_loop(0, n, lambda j, t: t + ball[j], jnp.zeros((1, LANES), F32))
 
     def apply(ball, d):
         s = match(ball)
@@ -317,16 +331,20 @@
         inv_ref[i] = c / determinant
     r0 = f_tod - unbin(solve(s1[:, 0:64], s1[:, 64:128], s1[:, 128:192]))
 
-    bin_out(ball2, r0, total(r0 * r0))
+    bin_out(ball2, sums2, r0, total(r0 * r0))
     start(ball2, 0)
+    start_direct(sums2, 2)
     finish(ball2, 0)
-    rr0 = scalar_of(ball2)
+    finish_direct(sums2, 2)
+    rr0 = gathered(sums2)[:, 0:1]
     q0 = apply(ball2, r0)
 
-    bin_out(ball3, q0, total(r0 * q0))
+    bin_out(ball3, sums3, q0, total(r0 * q0))
     start(ball3, 1)
+    start_direct(sums3, 3)
     finish(ball3, 1)
-    rq = scalar_of(ball3)
+    finish_direct(sums3, 3)
+    rq = gathered(sums3)[:, 0:1]
     w = apply(ball3, q0)
     alpha0 = rr0 / rq
     r1 = r0 - alpha0 * q0
@@ -340,7 +358,7 @@
     ball4[slot] = packed
     start_direct(ball4, 1)
     finish_direct(ball4, 1)
-    got = lax.fori_loop(0, n, lambda j, t: t + ball4[j], jnp.zeros((1, LANES), F32))
+    got = gathered(ball4)
     rr1 = got[0:1, 0:1]
     beta = rr1 / rr0
     d1 = r1 + beta * r0
@@ -372,15 +390,17 @@
                 pltpu.VMEM((6, ntile, BLK), F32),
                 pltpu.VMEM((n, 1, LANES), F32),
                 pltpu.VMEM((n, ntile, 8 * BLK), F32),
-                pltpu.VMEM((n, ntile, 4 * BLK), F32),
-                pltpu.VMEM((n, ntile, 4 * BLK), F32),
+                pltpu.VMEM((n, ntile + ntile // 2, 2 * BLK), F32),
+                pltpu.VMEM((n, ntile + ntile // 2, 2 * BLK), F32),
+                pltpu.VMEM((n, 1, LANES), F32),
+                pltpu.VMEM((n, 1, LANES), F32),
                 pltpu.VMEM((n, 1, LANES), F32),
                 pltpu.SemaphoreType.DMA((2,)),
                 pltpu.SemaphoreType.DMA((2, 4, nobs // 2)),
                 pltpu.SemaphoreType.DMA((2,)),
                 pltpu.SemaphoreType.DMA((2,)),
-                pltpu.SemaphoreType.DMA((2,)),
-                pltpu.SemaphoreType.DMA((2,)),
+                pltpu.SemaphoreType.DMA((4,)),
+                pltpu.SemaphoreType.DMA((4,)),
             ],
             compiler_params=pltpu.CompilerParams(
                 collective_id=0, has_side_effects=True, vmem_limit_bytes=60 * 1024 * 1024

time: 66.3 us -> 65.4 us (0.986)
  Pallas kernels: 64.2 us -> 63.3 us
    pallas_call x1, Pallas kernels: 64.2 us -> 63.3 us  [body(): pl.pallas_call(functools.partial(kernel, ndet, nobs), out_shape=jax.Shape...]
where the time goes in v3:
time: 65.4 us; the launch traced here: 65.2 us
  Pallas kernels  63.3 us (97%)
  local copies, waits for them, and re-layouts  1.25 us (2%)
    pallas_call x1, Pallas kernels, body(): pl.pallas_call(functools.partial(kernel, ndet, nobs), out_shape=jax.Shape...  63.3 us

profile of v3, /device:TPU:0, one launch (start us, length us, event | category | flops | bytes accessed | tf_op | source)
XLA Modules:
  0.0 65.2 jit_solution(10892781159269249706)
XLA Ops:
  0.6 63.3 %shard_map.77 = f32[2,40]{1,0:T(2,128)} custom-call(f32[64,128]{1,0:T(8,128)} %bitcast.9, f32[64,128]{1,0:T(8,128)} %bitcast.10, s32[64,128]{1,0:T(8,128)} %bitcast.11, s32[1,32]{1,0:T(1,128)} %bitcast.12, s32[1,40]{1,0:T(1,128)} %bitcast.13, s32[1,16]{1,0:T(1,128)} %touched_ref.1), custom_call_target="tpu_custom_call" | custom-call | tf_op jit(solution)/shard_map/pallas_call | solution.py:382
  63.9 1.3 %slice_bitcast_fusion = (f32[1,1,40]{2,1,0:T(1,128)}, f32[1,1,40]{2,1,0:T(1,128)}) fusion(f32[2,40]{1,0:T(2,128)} %shard_map.77), kind=kLoop, calls=%fused_computation | loop fusion | bytes 640 | tf_op jit(solution)/shard_map/reshape;squeeze | solution.py:416
